TPU v7x, 128 devices: a whole 4x4x4 slice. The times are simulated.
128 devices in a mesh: req: 8 (over x, core), exp: 16 (over y, z).
Axes of the slice: x: 4, y: 4, z: 4, core: 2. Of those that a mesh axis runs over, the one named last changes fastest.
Arguments:
- tokens: bfloat16 [16384, 2048], P(('req', 'exp')), may hold values from -6 to 6
- norm_gains: float32 [2, 2048], replicated, may hold values from 0.25 to 1.75
- w_query: bfloat16 [2048, 4, 2048], P(None, None, 'exp'), may hold values from -0.125 to 0.125
- w_keyval: bfloat16 [2048, 2, 2048], P(None, None, 'exp'), may hold values from -0.125 to 0.125
- w_out: bfloat16 [4, 2048, 2048], P(None, 'exp'), may hold values from -0.125 to 0.125
- page_pool: bfloat16 [32, 128, 16, 256], P('req', None, 'exp'), may hold values from -3000 to 3000
- page_dest: int32 [32], replicated, may hold values from 0 to 31, as said below
- prompt_lens: int32 [8, 4], P('req'), may hold values from 1 to 1024, 2048 in all within a row
- att_ids: int32 [16384, 2], P('req'), may hold values from 0 to 3, all different within a row
- att_gates: float32 [16384, 2], P('req'), may hold values from 0.1 to 1
- w_in: bfloat16 [2048, 2, 22528], P(None, None, 'exp'), may hold values from -0.125 to 0.125
- w_down: bfloat16 [22528, 2048], P('exp'), may hold values from -0.109375 to 0.109375
- moe_ids: int32 [16384, 2], P(('req', 'exp')), may hold values from 0 to 7, all different within a row; in each aligned block of 128 rows (0 to 127, 128 to 255, ...) at most 40 rows name the same one
- moe_gates: float32 [16384, 2], P(('req', 'exp')), may hold values from 0.1 to 1
- adapters: bfloat16 [64, 2, 16, 2048], P('exp'), may hold values from -0.25 to 0.25
- req_adapter: int32 [32], replicated, may hold values from 0 to 63, as said below
Outputs:
- layer_out: bfloat16 [16384, 2048], P(('req', 'exp'))
Inputs may be any that keep to these rules, and one draw needn't show every extreme that they name: `page_dest`: pool slot g * 4 + p holds the pages of request ((g + s_p) mod the number of groups) * 4 + p, where the 4 shifts s_p are distinct: a group's slots go to 4 different groups, and each group receives one request a slot. `prompt_lens`: the 4 lengths of a group sum to 2048. `att_ids`: the two ids of a token differ. `moe_ids`: the two ids of a token differ; among the 128 tokens of one device no expert is named by more than 40, a bound that some block reaches. `req_adapter`: exactly 16 distinct adapters are named, adapters 0 and 63 among them.
All inputs are finite; a program needn't handle non-finite values.
Results may differ from a plain program's by a relative error of at most 0.015.
Values may be sent and summed in bfloat16 or wider, within the bound.
A program may use at most 192 MiB of HBM per device.

v0:
```python
import math
import jax
import jax.numpy as jnp
from jax import lax
from jax.sharding import PartitionSpec as P

HD = 128
AEXP = 4
EXPERTS = 8
CACHE = 128
CAP = 40
norm_eps = 1e-05


def rms_scale(values, gain):
    values = values.astype(jnp.float32)
    factor = lax.rsqrt(jnp.mean(values * values, axis=-1, keepdims=True) + norm_eps)
    return (values * factor * gain).astype(jnp.bfloat16)


def rotate(vectors, places):
    half_width = vectors.shape[-1] // 2
    steps_idx = jnp.arange(half_width, dtype=jnp.float32)
    inverse = jnp.power(10000.0, steps_idx * (-2.0 / vectors.shape[-1]))
    angles = places.astype(jnp.float32)[:, None] * inverse[None, :]
    angles = angles.reshape((places.shape[0],) + (1,) * (vectors.ndim - 2) + (half_width,))
    cosine = jnp.cos(angles)
    sine_part = jnp.sin(angles)
    former = vectors[..., :half_width]
    latter = vectors[..., half_width:]
    return jnp.concatenate(
        [former * cosine - latter * sine_part, former * sine_part + latter * cosine], axis=-1
    )


def group_positions(lengths, total, cached):
    finish = jnp.cumsum(lengths)
    beginning = finish - lengths
    indices = jnp.arange(total, dtype=jnp.int32)
    segment = jnp.sum((indices[:, None] >= finish[None, :]).astype(jnp.int32), axis=1)
    member = segment[:, None] == jnp.arange(lengths.shape[0], dtype=jnp.int32)[None, :]
    offset = jnp.sum(jnp.where(member, beginning[None, :], 0), axis=1)
    return (segment, cached + indices - offset)


def attend_block(queries, key_rows, val_rows, visible, scale_factor):
    scores = (
        jnp.einsum("qhd,khd->hqk", queries, key_rows, preferred_element_type=jnp.float32)
        * scale_factor
    )
    scores = jnp.where(visible[None, :, :], scores, -1e30)
    highest = jnp.max(scores, axis=-1, keepdims=True)
    raised = jnp.exp(scores - highest)
    weights = (raised / jnp.sum(raised, axis=-1, keepdims=True)).astype(jnp.bfloat16)
    return jnp.einsum("hqk,khd->qhd", weights, val_rows, preferred_element_type=jnp.float32).astype(
        jnp.bfloat16
    )


def on_device(
    tokens,
    norm_gains,
    w_query,
    w_keyval,
    w_out,
    page_pool,
    page_dest,
    prompt_lens,
    att_ids,
    att_gates,
    w_in,
    w_down,
    moe_ids,
    moe_gates,
    adapters,
    req_adapter,
):
    groups = lax.axis_size("req")
    columns = lax.axis_size("exp")
    group_index = lax.axis_index("req")
    column_index = lax.axis_index("exp")
    tok_rows = tokens.shape[0]
    width = tokens.shape[1]
    group_rows = tok_rows * columns
    local_heads = w_query.shape[2] // HD
    slot_count = page_pool.shape[0]
    group_numbers = jnp.arange(groups, dtype=jnp.int32)
    own_target = (
        lax.dynamic_slice_in_dim(page_dest, group_index * slot_count, slot_count) // slot_count
    )
    outgoing_map = (own_target[None, :] == group_numbers[:, None]).astype(jnp.bfloat16)
    outgoing = jnp.dot(
        outgoing_map, page_pool.reshape(slot_count, -1), preferred_element_type=jnp.float32
    )
    outgoing = outgoing.astype(jnp.bfloat16).reshape((groups,) + page_pool.shape[1:])
    incoming = lax.all_to_all(outgoing, "req", split_axis=0, concat_axis=0, tiled=True)
    pool_slots = jnp.arange(page_dest.shape[0], dtype=jnp.int32)
    wanted = group_index * slot_count + jnp.arange(slot_count, dtype=jnp.int32)
    sender = (
        jnp.sum(jnp.where(page_dest[None, :] == wanted[:, None], pool_slots[None, :], 0), axis=1)
        // slot_count
    )
    incoming_map = (sender[:, None] == group_numbers[None, :]).astype(jnp.bfloat16)
    cached = jnp.dot(incoming_map, incoming.reshape(groups, -1), preferred_element_type=jnp.float32)
    cached = cached.astype(jnp.bfloat16).reshape(page_pool.shape)
    segment, places = group_positions(prompt_lens.reshape(-1), group_rows, CACHE)
    normed = rms_scale(tokens, norm_gains[0])
    gathered, factor_table = (
        lax.all_gather(normed, "exp", axis=0, tiled=True),
        lax.all_gather(adapters, "exp", axis=0, tiled=True),
    )
    queries = jnp.dot(gathered, w_query.reshape(width, -1), preferred_element_type=jnp.float32)
    queries = rotate(queries.reshape(group_rows, AEXP, local_heads, HD), places).astype(
        jnp.bfloat16
    )
    chosen_rows = (jnp.arange(group_rows, dtype=jnp.int32)[:, None] * AEXP + att_ids).reshape(-1)
    chosen = jnp.take(queries.reshape(group_rows * AEXP, local_heads * HD), chosen_rows, axis=0)
    keyval = jnp.dot(gathered, w_keyval.reshape(width, -1), preferred_element_type=jnp.float32)
    keyval = keyval.reshape(group_rows, 2, local_heads, HD)
    new_keys = rotate(keyval[:, 0], places).astype(jnp.bfloat16)
    new_values = keyval[:, 1].astype(jnp.bfloat16)
    key_rows = jnp.concatenate([cached[..., :HD].reshape(-1, local_heads, HD), new_keys], axis=0)
    val_rows = jnp.concatenate([cached[..., HD:].reshape(-1, local_heads, HD), new_values], axis=0)
    key_segment = jnp.concatenate(
        [jnp.repeat(jnp.arange(slot_count, dtype=jnp.int32), CACHE), segment]
    )
    key_index = jnp.concatenate(
        [jnp.full((slot_count * CACHE,), -1, jnp.int32), jnp.arange(group_rows, dtype=jnp.int32)]
    )
    query_total = 2 * group_rows
    block_rows = 1024
    block_count = query_total // block_rows
    query_segment = jnp.repeat(segment, 2).reshape(block_count, block_rows)
    query_index = jnp.repeat(jnp.arange(group_rows, dtype=jnp.int32), 2).reshape(
        block_count, block_rows
    )
    scale_factor = 1.0 / math.sqrt(HD)

    def block_step(items):
        block_queries, block_segment, block_index = items
        visible = (block_segment[:, None] == key_segment[None, :]) & (
            key_index[None, :] <= block_index[:, None]
        )
        return attend_block(block_queries, key_rows, val_rows, visible, scale_factor)

    heads_out = lax.map(
        block_step,
        (chosen.reshape(block_count, block_rows, local_heads, HD), query_segment, query_index),
    )
    heads_out = heads_out.reshape(group_rows, 2, local_heads * HD)
    slot_weights = jnp.where(
        att_ids[:, :, None] == jnp.arange(AEXP, dtype=jnp.int32)[None, None, :],
        att_gates[:, :, None],
        0.0,
    )
    mixed = jnp.einsum(
        "tje,tjx->tex", slot_weights, heads_out.astype(jnp.float32), precision=lax.Precision.HIGHEST
    ).astype(jnp.bfloat16)
    flat_mixed = mixed.reshape(group_rows, -1)
    flat_out = w_out.reshape(-1, width)
    attended = lax.psum_scatter(
        jnp.dot(flat_mixed, flat_out, preferred_element_type=jnp.float32).astype(jnp.bfloat16),
        "exp",
        scatter_dimension=0,
        tiled=True,
    ).astype(jnp.float32)
    hidden_state = (tokens.astype(jnp.float32) + attended).astype(jnp.bfloat16)
    hnorm = rms_scale(hidden_state, norm_gains[1])
    expert_flat = moe_ids.reshape(-1)
    expert_hits = (expert_flat[:, None] == jnp.arange(EXPERTS, dtype=jnp.int32)[None, :]).astype(
        jnp.int32
    )
    earlier = jnp.cumsum(expert_hits, axis=0) - expert_hits
    route_slot = jnp.sum(earlier * expert_hits, axis=1) + expert_flat * CAP
    table_size = EXPERTS * CAP
    placing = (jnp.arange(table_size, dtype=jnp.int32)[:, None] == route_slot[None, :]).reshape(
        table_size, tok_rows, 2
    )
    placing = jnp.any(placing, axis=2).astype(jnp.bfloat16)
    packed = jnp.dot(placing, hnorm, preferred_element_type=jnp.float32).astype(jnp.bfloat16)
    packed = packed.reshape(EXPERTS, CAP, width)
    copies = columns // EXPERTS
    spread_rows = jnp.repeat(packed, copies, axis=0)
    arrived = lax.all_to_all(spread_rows, "exp", split_axis=0, concat_axis=0, tiled=True)
    flat_rows = arrived.reshape(-1, width)
    gate_up = jnp.einsum("nd,dkf->nkf", flat_rows, w_in, preferred_element_type=jnp.float32)
    inner_act = (jax.nn.silu(gate_up[:, 0]) * gate_up[:, 1]).astype(jnp.bfloat16)
    partial_out = jnp.dot(inner_act, w_down, preferred_element_type=jnp.float32).reshape(
        columns, CAP, width
    )
    returned = lax.all_to_all(
        partial_out.astype(jnp.bfloat16), "exp", split_axis=0, concat_axis=0, tiled=True
    ).astype(partial_out.dtype)
    summed = jnp.sum(returned.reshape(EXPERTS, copies, CAP, width), axis=1).reshape(
        table_size, width
    )
    routed_rows = jnp.take(summed, route_slot, axis=0).reshape(tok_rows, 2, width)
    expert_out = jnp.sum(routed_rows * moe_gates[:, :, None], axis=1)
    own_segment = lax.dynamic_slice_in_dim(segment, column_index * tok_rows, tok_rows)
    wanted_ids = lax.dynamic_slice_in_dim(req_adapter, group_index * slot_count, slot_count)
    group_factors = jnp.take(factor_table, wanted_ids, axis=0)
    lowrank = jnp.einsum(
        "td,qrd->tqr", hnorm, group_factors[:, 0], preferred_element_type=jnp.float32
    )
    member = own_segment[:, None] == jnp.arange(slot_count, dtype=jnp.int32)[None, :]
    lowrank = jnp.where(member[:, :, None], lowrank, 0.0).astype(jnp.bfloat16)
    delta = jnp.einsum(
        "tqr,qrd->td", lowrank, group_factors[:, 1], preferred_element_type=jnp.float32
    )
    return (hidden_state.astype(jnp.float32) + expert_out + delta).astype(jnp.bfloat16)


def solution(mesh):
    in_specs = (
        P(("req", "exp"), None),
        P(),
        P(None, None, "exp"),
        P(None, None, "exp"),
        P(None, "exp", None),
        P("req", None, "exp", None),
        P(),
        P("req", None),
        P("req", None),
        P("req", None),
        P(None, None, "exp"),
        P("exp", None),
        P(("req", "exp"), None),
        P(("req", "exp"), None),
        P("exp", None, None, None),
        P(),
    )
    out_specs = P(("req", "exp"), None)
    return jax.shard_map(
        on_device, mesh=mesh, in_specs=in_specs, out_specs=out_specs, check_vma=False
    )
```

profile of v0, /device:TPU:16, one launch (start us, length us, event | category | flops | bytes accessed | tf_op | source)
XLA Modules:
  0.0 430.3 jit_solution(572273095030612041)
XLA Ops:
  6.5 1.5 fusion.81
  8.0 1.2 fusion.34
  9.3 2.0 fusion.36
  11.3 1.2 copy.147
  12.9 0.9 copy.128
  13.8 4.4 %all-to-all-start = ((bf16[8,128,1,256]{3,1,2,0:T(8,128)(2,1)}), bf16[8,128,1,256]{3,1,2,0:T(8,128)(2,1)}, u32[]{:S(2)}, u32[]{:S(2)}) async-start(bf16[8,128,1,256]{3,1,2,0:T(8,128)(2,1)} %copy.128), calls=%async_computation | async-start | bytes 1048576 | tf_op jit(solution)/shard_map/all_to_all | solution.py:96
  19.9 1.4 copy.119
  21.5 3.3 copy.159
  24.8 4.3 copy.123
  29.1 1.4 copy.160
  30.4 1.4 copy.130
  32.3 0.8 copy.132
  33.7 1.4 copy.120
  37.3 2.8 multiply_cosine_fusion.1
  40.1 1.3 copy.148
  42.1 42.5 %all-gather.3.cloned.1.call-done = bf16[2048,2048]{1,0:T(8,128)(2,1)} async-done(((bf16[128,2048]{1,0:T(8,128)(2,1)}), bf16[2048,2048]{1,0:T(8,128)(2,1)}) %all-gather.3.cloned.1.call-update) | async-done | bytes 8388624 | tf_op jit(solution)/shard_map/all_gather | solution.py:109
  84.6 5.9 %fusion.24 = f32[2048,2,1,128]{0,3,1,2:T(8,128)S(1)} fusion(bf16[2,128,2048]{2,1,0:T(8,128)(2,1)S(1)} %bitcast.178, bf16[2048,2048]{1,0:T(8,128)(2,1)} %all-gather.3.cloned.1.call-done), kind=kOutput, calls=%fused_computation.34 | convolution fusion | flops 2147483648 | bytes 11534336 | tf_op jit(solution)/shard_map/dot_general | solution.py:118
  90.5 1.1 slice_bitcast_fusion
  91.6 0.9 fusion.52
  92.5 4.5 %fusion.18 = f32[2048,4,1,128]{0,3,1,2:T(8,128)S(1)} fusion(bf16[4,128,2048]{2,1,0:T(8,128)(2,1)S(1)} %bitcast.173, bf16[2048,2048]{1,0:T(8,128)(2,1)S(1)} %copy-done.22), kind=kOutput, calls=%fused_computation.32 | convolution fusion | flops 4294967296 | bytes 14680064 | tf_op jit(solution)/shard_map/dot_general | solution.py:112
  97.1 1.7 subtract_convert_fusion
  98.8 4.1 copy.124
  102.8 2.5 copy.125
  105.3 4.3 %fusion.49 = (bf16[2048,1,64]{0,2,1:T(8,128)(2,1)S(1)}, bf16[2048,1,64]{0,2,1:T(8,128)(2,1)S(1)}) fusion(f32[2048,1,128]{0,2,1:T(8,128)} %slice_bitcast_fusion, f32[64]{0:T(128)} %copy-done.19, f32[2048]{0:T(1024)} %copy-done.11), kind=kLoop, calls=%fused_computation.81 | loop fusion | flops 1179648 | bytes 1581312 | tf_op jit(solution)/shard_map/convert.2
  109.7 1.1 copy.133
  110.8 1.1 copy.134
  111.9 4.7 %pad_maximum_fusion = bf16[8192,128]{1,0:T(8,128)(2,1)} fusion(bf16[8192,64]{1,0:T(8,128)(2,1)} %bitcast.164, bf16[8192,64]{1,0:T(8,128)(2,1)} %bitcast.163), kind=kLoop, calls=%fused_computation.40 | loop fusion | flops 4194304 | bytes 4194304 | tf_op jit(solution)/shard_map/concatenate | solution.py:31
  116.6 12.9 %gather_fusion = bf16[4096,128]{1,0:T(8,128)(2,1)S(1)} fusion(bf16[8192,128]{1,0:T(8,128)(2,1)} %pad_maximum_fusion, s32[4096]{0:T(1024)S(1)} %copy-done.14), kind=kCustom, calls=%fused_computation | custom fusion | bytes 2113536 | tf_op jit(solution)/shard_map/jit(_take)/gather | solution.py:117
  129.6 2.1 broadcast_select_fusion
  131.7 36.9 %while.11 = (s32[]{:T(128)}, bf16[4,1024,1,128]{3,1,2,0:T(8,128)(2,1)}, s32[4,1024]{1,0:T(4,128)}, s32[2560]{0:T(1024)S(1)}, s32[4,1024]{1,0:T(4,128)S(1)}, /*in...) while((s32[]{:T(128)}, ...), condition=%wide.region_8.9_spmd, body=%wide.region_5.8_spmd.sunk | while | flops 1371142144 | bytes 35980420 | solution.py:146
  131.7 0.8 constant_dynamic-slice_fusion.3
  132.6 4.0 fusion.96
  136.6 1.6 fusion.97
  138.2 2.9 fusion.98
  141.0 0.7 constant_dynamic-slice_fusion.3
  141.8 4.0 fusion.96
  145.8 1.6 fusion.97
  147.4 2.9 fusion.98
  150.2 0.7 constant_dynamic-slice_fusion.3
  151.0 4.0 fusion.96
  155.0 1.6 fusion.97
  156.6 2.9 fusion.98
  159.5 0.7 constant_dynamic-slice_fusion.3
  160.2 4.0 fusion.96
  164.2 1.6 fusion.97
  165.8 2.9 fusion.98
  168.7 14.3 %fusion.31 = bf16[2048,4,128]{2,1,0:T(4,128)(2,1)S(1)} fusion(bf16[2048,2,128]{2,1,0:T(2,128)(2,1)} %bitcast.33, f32[2048,2]{1,0:T(8,128)} %copy.120, s32[2048,2]{1,0:T(8,128)S(1)} %copy-done.7), kind=kOutput, calls=%fused_computation.46 | convolution fusion | flops 26247168 | bytes 3178496 | tf_op jit(solution)/shard_map/tje,tjx->tex/dot_general | solution.py:156
  183.0 6.5 %bitcast_convert_fusion = bf16[2048,2048]{1,0:T(8,128)(2,1)} fusion(bf16[4,128,2048]{2,1,0:T(8,128)(2,1)S(1)} %copy-done, bf16[2048,4,128]{2,1,0:T(4,128)(2,1)S(1)} %fusion.31), kind=kOutput, calls=%fused_computation.20 | convolution fusion | flops 4299161600 | bytes 12582912 | tf_op jit(solution)/shard_map/dot_general | solution.py:162
  191.9 83.4 %reduce-scatter.2.cloned.1.call-done = bf16[128,2048]{1,0:T(8,128)(2,1)} async-done(((bf16[2048,2048]{1,0:T(8,128)(2,1)}), bf16[128,2048]{1,0:T(8,128)(2,1)}) %reduce-scatter.2.cloned.1.call-update) | async-done | bytes 524304 | tf_op jit(solution)/shard_map/reduce_scatter | solution.py:161
  275.4 1.3 fusion.38
  276.7 1.6 convolution_convert_fusion.2
  278.6 44.5 %all_to_all.15 = bf16[16,40,2048]{2,1,0:T(8,128)(2,1)S(1)} all-to-all(bf16[16,40,2048]{2,1,0:T(8,128)(2,1)S(1)} %bitcast.162), channel_id=1, replica_groups=mesh['req'=8,'exp'=16] {'exp'}, dimensions={0} | all-to-all | bytes 5242880 | tf_op jit(solution)/shard_map/all_to_all | solution.py:184
  323.2 11.9 %fusion.10 = f32[640,2,1408]{2,0,1:T(8,128)S(1)} fusion(bf16[640,2048,1]{1,0,2:T(8,128)(2,1)S(1)} %bitcast.171, bf16[2048,2,1408]{2,1,0:T(2,128)(2,1)} %param.28), kind=kOutput, calls=%fused_computation.21 | convolution fusion | flops 7381975040 | bytes 21364736 | tf_op jit(solution)/shard_map/nd,dkf->nkf/dot_general | solution.py:186
  335.6 6.1 %fusion.21 = bf16[16,40,2048]{2,1,0:T(8,128)(2,1)} fusion(bf16[1408,2048]{1,0:T(8,128)(2,1)S(1)} %bitcast.195, f32[16,40,1408]{2,1,0:T(8,128)S(1)} %bitcast.170, f32[16,40,1408]{2,1,0:T(8,128)S(1)} %bitcast.169), kind=kOutput, calls=%fused_computation.33 | convolution fusion | flops 3697704960 | bytes 15597568 | tf_op jit(solution)/shard_map/dot_general | solution.py:188
  341.7 7.0 %all-to-all-start.2 = ((bf16[16,40,2048]{2,1,0:T(8,128)(2,1)}), bf16[16,40,2048]{2,1,0:T(8,128)(2,1)}, u32[]{:S(2)}, u32[]{:S(2)}) async-start(bf16[16,40,2048]{2,1,0:T(8,128)(2,1)} %fusion.21), calls=%async_computation.3 | async-start | bytes 5242880 | tf_op jit(solution)/shard_map/all_to_all | solution.py:191
  349.2 0.8 dynamic_slice.27
  350.1 45.9 %all-gather.5.cloned.1.call-done = bf16[64,2,16,2048]{3,2,1,0:T(8,128)(2,1)} async-done(((bf16[4,2,16,2048]{3,2,1,0:T(8,128)(2,1)}), bf16[64,2,16,2048]{3,2,1,0:T(8,128)(2,1)}) %all-gather.5.cloned.1.call-update) | async-done | bytes 8388624 | tf_op jit(solution)/shard_map/all_gather | solution.py:110
  395.9 4.0 gather_fusion.2
  399.9 0.9 copy_select_fusion
  400.8 4.1 convert_reduce_fusion
  404.9 5.3 %gather_fusion.1 = f32[256,2048]{1,0:T(8,128)} fusion(f32[320,2048]{1,0:T(8,128)} %bitcast.161, s32[1024]{0:T(1024)S(1)} %pad_clamp_fusion.1), kind=kCustom, calls=%fused_computation.1 | custom fusion | bytes 4195328 | tf_op jit(solution)/shard_map/jit(_take)/gather | solution.py:197
  410.3 3.5 gather.19
  413.8 6.6 %multiply_reduce_fusion = f32[128,2048]{1,0:T(8,128)} fusion(f32[128,2,2048]{2,1,0:T(2,128)} %gather.19, pred[128,2]{1,0:T(8,128)(4,1)S(1)} %copy.139, f32[128,2]{1,0:T(8,128)S(1)} %copy.142), kind=kLoop, calls=%fused_computation.42 | loop fusion | flops 1310720 | bytes 3147008 | tf_op jit(solution)/shard_map/reduce_sum | solution.py:198
  420.4 3.1 fusion.28
  (132 shorter events, 10.0 us)
Async XLA Ops:
  6.5 176.4 %copy-start = (bf16[4,128,2048]{2,1,0:T(8,128)(2,1)S(1)}, bf16[4,128,2048]{2,1,0:T(8,128)(2,1)}, u32[]{:S(2)}) copy-start(bf16[4,128,2048]{2,1,0:T(8,128)(2,1)} %param.22) | copy-start | bytes 6291460
  6.5 6.0 %copy-start.23 = (s32[32]{0:T(128)S(1)}, s32[32]{0:T(128)}, u32[]{:S(2)}) copy-start(s32[32]{0:T(128)} %param.24) | copy-start | bytes 388
  6.5 78.1 %all-gather.3.cloned.1.call-start = ((), (), s32[]{:S(2)}) async-start(), calls=%async_computation.4 | async-start | bytes 8912896 | tf_op jit(solution)/shard_map/all_gather | solution.py:109
  9.3 9.0 %copy-start.13 = (s32[2048,2]{0,1:T(2,128)S(1)}, s32[2048,2]{0,1:T(2,128)}, u32[]{:S(2)}) copy-start(s32[2048,2]{0,1:T(2,128)} %param.26) | copy-start | bytes 49156
  13.8 7.5 %copy-start.24 = (s32[1,4]{1,0:T(1,128)S(1)}, s32[1,4]{1,0:T(1,128)}, u32[]{:S(2)}) copy-start(s32[1,4]{1,0:T(1,128)} %param.25) | copy-start | bytes 52
  13.8 26.3 %all-to-all-start = ((bf16[8,128,1,256]{3,1,2,0:T(8,128)(2,1)}), bf16[8,128,1,256]{3,1,2,0:T(8,128)(2,1)}, u32[]{:S(2)}, u32[]{:S(2)}) async-start(bf16[8,128,1,256]{3,1,2,0:T(8,128)(2,1)} %copy.128), calls=%async_computation | async-start | bytes 1048576 | tf_op jit(solution)/shard_map/all_to_all | solution.py:96
  18.2 257.1 %reduce-scatter.2.cloned.1.call-start = ((), (), s32[]{:S(2)}) async-start(), calls=%async_computation.5 | async-start | bytes 8912896 | tf_op jit(solution)/shard_map/reduce_scatter | solution.py:161
  30.4 3.3 copy-start.15
  32.0 8.1 %copy-start.10 = (s32[2048]{0:T(1024)}, s32[2048]{0:T(1024)S(1)}, u32[]{:S(2)}) copy-start(s32[2048]{0:T(1024)S(1)} %convert_reduce_fusion.1) | copy-start | bytes 24580
  33.7 50.9 %copy-start.8 = (bf16[256,2048]{1,0:T(8,128)(2,1)S(1)}, bf16[256,2048]{1,0:T(8,128)(2,1)}, u32[]{:S(2)}) copy-start(bf16[256,2048]{1,0:T(8,128)(2,1)} %copy.130) | copy-start | bytes 3145732
  35.1 6.7 %copy-start.19 = (f32[64]{0:T(128)}, f32[64]{0:T(128)S(1)}, u32[]{:S(2)}) copy-start(f32[64]{0:T(128)S(1)} %multiply_power_fusion) | copy-start | bytes 772
  36.0 5.8 %copy-start.11 = (f32[2048]{0:T(1024)}, f32[2048]{0:T(1024)S(1)}, u32[]{:S(2)}) copy-start(f32[2048]{0:T(1024)S(1)} %subtract_convert_fusion.1) | copy-start | bytes 24580
  84.6 7.8 %copy-start.22 = (bf16[2048,2048]{1,0:T(8,128)(2,1)S(1)}, bf16[2048,2048]{1,0:T(8,128)(2,1)}, u32[]{:S(2)}) copy-start(bf16[2048,2048]{1,0:T(8,128)(2,1)} %all-gather.3.cloned.1.call-done) | copy-start | bytes 25165828
  90.5 2.0 copy-start.5
  92.5 4.5 %copy-start.3 = (f32[2048,64]{0,1:T(8,128)S(1)}, f32[2048,64]{0,1:T(8,128)}, u32[]{:S(2)}) copy-start(f32[2048,64]{0,1:T(8,128)} %get-tuple-element.159) | copy-start | bytes 1572868
  92.5 4.5 %copy-start.4 = (f32[2048,64]{0,1:T(8,128)S(1)}, f32[2048,64]{0,1:T(8,128)}, u32[]{:S(2)}) copy-start(f32[2048,64]{0,1:T(8,128)} %get-tuple-element.160) | copy-start | bytes 1572868
  105.3 5.5 %copy-start.6 = (bf16[2048,1,128]{0,2,1:T(8,128)(2,1)S(1)}, bf16[2048,1,128]{0,2,1:T(8,128)(2,1)}, u32[]{:S(2)}) copy-start(bf16[2048,1,128]{0,2,1:T(8,128)(2,1)} %fusion.52) | copy-start | bytes 1572868
  111.9 4.7 %copy-start.14 = (s32[4096]{0:T(1024)S(1)}, s32[4096]{0:T(1024)}, u32[]{:S(2)}) copy-start(s32[4096]{0:T(1024)} %broadcast_clamp_fusion) | copy-start | bytes 49156
  116.6 13.0 %copy-start.16 = (pred[4,1024]{1,0:T(4,128)(4,1)S(1)}, pred[4,1024]{1,0:T(4,128)(4,1)}, u32[]{:S(2)}) copy-start(pred[4,1024]{1,0:T(4,128)(4,1)} %compare_and_fusion) | copy-start | bytes 12292
  116.6 15.1 %copy-start.17 = (s32[2560]{0:T(1024)S(1)}, s32[2560]{0:T(1024)}, u32[]{:S(2)}) copy-start(s32[2560]{0:T(1024)} %pad_add_fusion) | copy-start | bytes 30724
  116.6 15.1 %copy-start.25 = (s32[2560]{0:T(1024)S(1)}, s32[2560]{0:T(1024)}, u32[]{:S(2)}) copy-start(s32[2560]{0:T(1024)} %constant.115.clone.1) | copy-start | bytes 30724
  131.7 36.9 %copy-start.7 = (s32[2048,2]{1,0:T(8,128)S(1)}, s32[2048,2]{1,0:T(8,128)}, u32[]{:S(2)}) copy-start(s32[2048,2]{1,0:T(8,128)} %copy.119) | copy-start | bytes 49156
  136.6 1.6 copy-start.9
  145.8 1.6 copy-start.9
  155.0 1.6 copy-start.9
  164.2 1.6 copy-start.9
  189.5 0.8 copy-start.18
  189.5 85.8 %copy-start.1 = (bf16[128,2048]{1,0:T(8,128)(2,1)S(1)}, bf16[128,2048]{1,0:T(8,128)(2,1)}, u32[]{:S(2)}) copy-start(bf16[128,2048]{1,0:T(8,128)(2,1)} %param.18) | copy-start | bytes 1572868
  189.5 87.2 %copy-start.12 = (f32[1,2048]{1,0:T(1,128)S(1)}, f32[1,2048]{1,0:T(1,128)}, u32[]{:S(2)}) copy-start(f32[1,2048]{1,0:T(1,128)} %get-tuple-element.158) | copy-start | bytes 24580
  189.5 206.4 %all-gather.5.cloned.1.call-start = ((), (), s32[]{:S(2)}) async-start(), calls=%async_computation.6 | async-start | bytes 8912896 | tf_op jit(solution)/shard_map/all_gather | solution.py:110
  278.6 57.0 %slice-start = ((s8[5767168]{0:T(1024)(128)(4,1)}), s8[4194304]{0:T(1024)(128)(4,1)S(1)}, s32[]{:S(2)}) async-start(s8[5767168]{0:T(1024)(128)(4,1)} %bitcast.194), calls=%async_computation.7 | async-start | bytes 8388608
  323.2 12.4 %slice-start.1 = ((s8[5767168]{0:T(1024)(128)(4,1)}), s8[1572864]{0:T(1024)(128)(4,1)S(1)}, s32[]{:S(2)}) async-start(s8[5767168]{0:T(1024)(128)(4,1)} %bitcast.194), calls=%async_computation.8 | async-start | bytes 3145728
  341.7 7.4 %copy-start.20 = (f32[128,2]{0,1:T(2,128)S(1)}, f32[128,2]{0,1:T(2,128)}, u32[]{:S(2)}) copy-start(f32[128,2]{0,1:T(2,128)} %param.31) | copy-start | bytes 3076
  341.7 8.3 %copy-start.21 = (s32[32]{0:T(128)S(1)}, s32[32]{0:T(128)}, u32[]{:S(2)}) copy-start(s32[32]{0:T(128)} %param.33) | copy-start | bytes 388
  341.7 59.1 %all-to-all-start.2 = ((bf16[16,40,2048]{2,1,0:T(8,128)(2,1)}), bf16[16,40,2048]{2,1,0:T(8,128)(2,1)}, u32[]{:S(2)}, u32[]{:S(2)}) async-start(bf16[16,40,2048]{2,1,0:T(8,128)(2,1)} %fusion.21), calls=%async_computation.3 | async-start | bytes 5242880 | tf_op jit(solution)/shard_map/all_to_all | solution.py:191
  413.8 6.6 %copy-start.2 = (bf16[128,2048]{1,0:T(8,128)(2,1)S(1)}, bf16[128,2048]{1,0:T(8,128)(2,1)}, u32[]{:S(2)}) copy-start(bf16[128,2048]{1,0:T(8,128)(2,1)} %reduce-scatter.2.cloned.1.call-done) | copy-start | bytes 1572868
Sparse Core Ops, SparseCore 0:
  11.5 73.1 all-gather.2
  189.7 85.6 reduce-scatter.1
  277.5 118.3 all-gather.4
where the time goes:
time: 435 us; the launch traced here: 430 us
  waiting for transfers between devices  173 us (40%)
  matrix products  82.2 us (19%)
  local copies, waits for them, and re-layouts  64 us (15%)
  blocking collectives  44.5 us (10%)
  other arithmetic  41.6 us (10%)
  between operations  13.9 us (3%)
  starting transfers between devices  11.5 us (3%)
    reduce_scatter x1, waiting for transfers between devices, on_device(): lax.psum_scatter(jnp.dot(flat_mixed, flat_out, preferred_element_type=jnp...  83.4 us
    all_gather x1, waiting for transfers between devices, on_device(): lax.all_gather(adapters, 'exp', axis=0, tiled=True)  45.9 us
    all_to_all x1, blocking collectives, on_device(): lax.all_to_all(spread_rows, 'exp', split_axis=0, concat_axis=0, tiled=True)  44.5 us
    all_gather x1, waiting for transfers between devices, on_device(): lax.all_gather(normed, 'exp', axis=0, tiled=True)  42.5 us
    dot_general x4, matrix products, attend_block(): jnp.einsum('qhd,khd->hqk', queries, key_rows, preferred_element_type=jnp....  16.1 us
    dot_general x1, matrix products, on_device(): jnp.einsum('tje,tjx->tex', slot_weights, heads_out.astype(jnp.float32), p...  14.3 us
    gather x1, local copies, waits for them, and re-layouts, on_device(): jnp.take(queries.reshape(group_rows * AEXP, local_heads * HD), chosen_row...  12.9 us
    dot_general x1, matrix products, on_device(): jnp.einsum('nd,dkf->nkf', flat_rows, w_in, preferred_element_type=jnp.flo...  11.9 us
  transfers between devices with their start and end apart: 5, of which 3 were waited for; matrix products, arithmetic and copies ran while one was open for 13% of the time, Pallas kernels for 0%

commit v1 on v0

--- a/solution.py
+++ b/solution.py
@@ -3,6 +3,7 @@
 import jax.numpy as jnp
 from jax import lax
 from jax.sharding import PartitionSpec as P
+from jax.lax import all_to_all, psum
 
 HD = 128
 AEXP = 4
@@ -75,6 +76,14 @@
     adapters,
     req_adapter,
 ):
+
+    def divide_sections(field, which_axis, in_dim):
+        kept_arr = jnp.stack(tuple((field for _ in range(psum(1, axis_name=which_axis)))))
+        ready = jnp.concatenate(
+            all_to_all(kept_arr, concat_axis=0, axis_name=which_axis, split_axis=0), axis=in_dim
+        )
+        return ready
+
     groups = lax.axis_size("req")
     columns = lax.axis_size("exp")
     group_index = lax.axis_index("req")
@@ -107,7 +116,7 @@
     normed = rms_scale(tokens, norm_gains[0])
     gathered, factor_table = (
         lax.all_gather(normed, "exp", axis=0, tiled=True),
-        lax.all_gather(adapters, "exp", axis=0, tiled=True),
+        divide_sections(adapters, which_axis="exp", in_dim=0),
     )
     queries = jnp.dot(gathered, w_query.reshape(width, -1), preferred_element_type=jnp.float32)
     queries = rotate(queries.reshape(group_rows, AEXP, local_heads, HD), places).astype(

time: 435 us -> 528 us (1.21)
  the two profiles are of different devices: /device:TPU:16 before, /device:TPU:4 now
where the time goes in v1:
time: 528 us; the launch traced here: 523 us
  waiting for transfers between devices  256 us (48%)
  matrix products  85.6 us (16%)
  local copies, waits for them, and re-layouts  69 us (13%)
  other arithmetic  41.6 us (8%)
  blocking collectives  37.4 us (7%)
  starting transfers between devices  19.5 us (4%)
  between operations  14.1 us (3%)
    all_to_all x1, waiting for transfers between devices, divide_sections(): all_to_all(kept_arr, concat_axis=0, axis_name=which_axis, split_axis=0)  105 us
    reduce_scatter x1, waiting for transfers between devices, on_device(): lax.psum_scatter(jnp.dot(flat_mixed, flat_out, preferred_element_type=jnp...  83.5 us
    all_gather x1, waiting for transfers between devices, on_device(): lax.all_gather(normed, 'exp', axis=0, tiled=True)  42.1 us
    all_to_all x1, blocking collectives, on_device(): lax.all_to_all(spread_rows, 'exp', split_axis=0, concat_axis=0, tiled=True)  37.4 us
    all_to_all x1, waiting for transfers between devices, on_device(): lax.all_to_all(partial_out.astype(jnp.bfloat16), 'exp', split_axis=0, con...  25.1 us
    dot_general x4, matrix products, attend_block(): jnp.einsum('qhd,khd->hqk', queries, key_rows, preferred_element_type=jnp....  16 us
    dot_general x1, matrix products, on_device(): jnp.einsum('tje,tjx->tex', slot_weights, heads_out.astype(jnp.float32), p...  14.3 us
    gather x1, local copies, waits for them, and re-layouts, on_device(): jnp.take(queries.reshape(group_rows * AEXP, local_heads * HD), chosen_row...  12.9 us
  transfers between devices with their start and end apart: 5, of which 4 were waited for; matrix products, arithmetic and copies ran while one was open for 11% of the time, Pallas kernels for 0%

profile of v1, /device:TPU:4, one launch (start us, length us, event | category | flops | bytes accessed | tf_op | source)
XLA Modules:
  0.0 523.3 jit_solution(15234287241469977093)
XLA Ops:
  6.5 1.5 fusion.81
  8.0 1.2 fusion.34
  9.3 2.0 fusion.36
  11.3 1.2 copy.147
  12.9 0.9 copy.128
  13.8 4.9 all-to-all-start
  20.3 1.4 copy.119
  22.4 0.8 copy.132
  23.8 3.3 copy.159
  27.1 4.3 copy.123
  31.4 1.4 copy.160
  32.8 1.4 copy.130
  34.2 1.4 copy.120
  37.8 2.8 multiply_cosine_fusion.1
  40.6 1.3 copy.148
  42.6 42.1 %all-gather.2.cloned.1.call-done = bf16[2048,2048]{1,0:T(8,128)(2,1)} async-done(((bf16[128,2048]{1,0:T(8,128)(2,1)}), bf16[2048,2048]{1,0:T(8,128)(2,1)}) %all-gather.2.cloned.1.call-update) | async-done | bytes 8388624 | tf_op jit(solution)/shard_map/all_gather | solution.py:118
  84.8 5.9 %fusion.24 = f32[2048,2,1,128]{0,3,1,2:T(8,128)S(1)} fusion(bf16[2,128,2048]{2,1,0:T(8,128)(2,1)S(1)} %bitcast.179, bf16[2048,2048]{1,0:T(8,128)(2,1)} %all-gather.2.cloned.1.call-done), kind=kOutput, calls=%fused_computation.34 | convolution fusion | flops 2147483648 | bytes 11534336 | tf_op jit(solution)/shard_map/dot_general | solution.py:127
  90.7 1.0 slice_bitcast_fusion
  91.7 0.9 fusion.52
  92.6 4.5 fusion.18
  97.2 1.7 subtract_convert_fusion
  98.9 4.1 copy.125
  102.9 2.5 copy.124
  105.4 4.3 fusion.49
  109.8 1.1 copy.133
  111.0 1.1 copy.134
  112.1 4.7 pad_maximum_fusion
  116.8 12.9 %gather_fusion = bf16[4096,128]{1,0:T(8,128)(2,1)S(1)} fusion(bf16[8192,128]{1,0:T(8,128)(2,1)} %pad_maximum_fusion, s32[4096]{0:T(1024)S(1)} %copy-done.15), kind=kCustom, calls=%fused_computation | custom fusion | bytes 2113536 | tf_op jit(solution)/shard_map/jit(_take)/gather | solution.py:126
  129.7 2.1 broadcast_select_fusion
  131.9 37.0 %while.11 = (s32[]{:T(128)}, bf16[4,1024,1,128]{3,1,2,0:T(8,128)(2,1)}, s32[4,1024]{1,0:T(4,128)}, s32[2560]{0:T(1024)S(1)}, s32[4,1024]{1,0:T(4,128)S(1)}, /*in...) while((s32[]{:T(128)}, ...), condition=%wide.region_8.9_spmd, body=%wide.region_5.8_spmd.sunk | while | flops 1371142144 | bytes 35979412 | solution.py:155
  131.9 0.8 constant_dynamic-slice_fusion.3
  132.7 4.0 fusion.96
  136.7 1.6 fusion.97
  138.3 2.9 fusion.98
  141.9 4.0 fusion.96
  145.9 1.6 fusion.97
  147.5 2.9 fusion.98
  151.1 4.0 fusion.96
  155.2 1.6 fusion.97
  156.7 2.9 fusion.98
  160.4 4.0 fusion.96
  164.4 1.6 fusion.97
  166.0 2.9 fusion.98
  168.8 14.3 %fusion.31 = bf16[2048,4,128]{2,1,0:T(4,128)(2,1)S(1)} fusion(bf16[2048,2,128]{2,1,0:T(2,128)(2,1)} %bitcast.196, f32[2048,2]{1,0:T(8,128)} %copy.120, s32[2048,2]{1,0:T(8,128)S(1)} %copy-done.7), kind=kOutput, calls=%fused_computation.46 | convolution fusion | flops 26247168 | bytes 3178496 | tf_op jit(solution)/shard_map/tje,tjx->tex/dot_general | solution.py:165
  183.2 6.6 %bitcast_convert_fusion = bf16[2048,2048]{1,0:T(8,128)(2,1)} fusion(bf16[4,128,2048]{2,1,0:T(8,128)(2,1)S(1)} %copy-done, bf16[2048,4,128]{2,1,0:T(4,128)(2,1)S(1)} %fusion.31), kind=kOutput, calls=%fused_computation.20 | convolution fusion | flops 4299161600 | bytes 12582912 | tf_op jit(solution)/shard_map/dot_general | solution.py:171
  192.0 83.5 %reduce-scatter.2.cloned.1.call-done = bf16[128,2048]{1,0:T(8,128)(2,1)} async-done(((bf16[2048,2048]{1,0:T(8,128)(2,1)}), bf16[128,2048]{1,0:T(8,128)(2,1)}) %reduce-scatter.2.cloned.1.call-update) | async-done | bytes 524304 | tf_op jit(solution)/shard_map/reduce_scatter | solution.py:170
  275.5 1.3 fusion.38
  276.8 1.6 convolution_convert_fusion.2
  278.8 37.4 %all_to_all.20 = bf16[16,40,2048]{2,1,0:T(8,128)(2,1)} all-to-all(bf16[16,40,2048]{2,1,0:T(8,128)(2,1)S(1)} %bitcast.163), channel_id=1, replica_groups=mesh['req'=8,'exp'=16] {'exp'}, dimensions={0} | all-to-all | bytes 5242880 | tf_op jit(solution)/shard_map/all_to_all | solution.py:193
  316.2 4.3 stack.2
  320.5 5.0 all-to-all-start.3
  325.5 12.8 %fusion.10 = f32[640,2,1408]{2,0,1:T(8,128)S(1)} fusion(bf16[640,2048,1]{1,0,2:T(8,128)(2,1)} %bitcast.172, bf16[2048,2,1408]{2,1,0:T(2,128)(2,1)} %param.28), kind=kOutput, calls=%fused_computation.21 | convolution fusion | flops 7381975040 | bytes 21364736 | tf_op jit(solution)/shard_map/nd,dkf->nkf/dot_general | solution.py:195
  338.8 8.5 %fusion.21 = bf16[16,40,2048]{2,1,0:T(8,128)(2,1)} fusion(bf16[1408,2048]{1,0:T(8,128)(2,1)} %param.29, f32[16,40,1408]{2,1,0:T(8,128)S(1)} %bitcast.171, f32[16,40,1408]{2,1,0:T(8,128)S(1)} %bitcast.170), kind=kOutput, calls=%fused_computation.33 | convolution fusion | flops 3697704960 | bytes 15597568 | tf_op jit(solution)/shard_map/dot_general | solution.py:197
  347.3 105.4 %all-to-all-done.3 = bf16[16,4,2,16,2048]{4,3,2,1,0:T(8,128)(2,1)} async-done(((bf16[16,4,2,16,2048]{4,3,2,1,0:T(8,128)(2,1)}), bf16[16,4,2,16,2048]{4,3,2,1,0:T(8,128)(2,1)}, u32[]{:S(2)}, u32[]{:S(2)}) %all-to-all-start.3) | async-done | bytes 8388640 | tf_op jit(solution)/shard_map/all_to_all | solution.py:83
  452.7 9.6 %all-to-all-start.2 = ((bf16[16,40,2048]{2,1,0:T(8,128)(2,1)}), bf16[16,40,2048]{2,1,0:T(8,128)(2,1)}, u32[]{:S(2)}, u32[]{:S(2)}) async-start(bf16[16,40,2048]{2,1,0:T(8,128)(2,1)} %fusion.21), calls=%async_computation.3 | async-start | bytes 5242880 | tf_op jit(solution)/shard_map/all_to_all | solution.py:200
  462.8 0.8 dynamic_slice.27
  463.6 4.0 gather_fusion.2
  467.6 0.9 copy_select_fusion
  468.5 25.1 %all-to-all-done.2 = bf16[16,40,2048]{2,1,0:T(8,128)(2,1)} async-done(((bf16[16,40,2048]{2,1,0:T(8,128)(2,1)}), bf16[16,40,2048]{2,1,0:T(8,128)(2,1)}, u32[]{:S(2)}, u32[]{:S(2)}) %all-to-all-start.2) | async-done | bytes 2621472 | tf_op jit(solution)/shard_map/all_to_all | solution.py:200
  493.6 4.1 convert_reduce_fusion
  497.7 5.4 %gather_fusion.1 = f32[256,2048]{1,0:T(8,128)} fusion(f32[320,2048]{1,0:T(8,128)} %bitcast.162, s32[1024]{0:T(1024)S(1)} %pad_clamp_fusion.1), kind=kCustom, calls=%fused_computation.1 | custom fusion | bytes 4195328 | tf_op jit(solution)/shard_map/jit(_take)/gather | solution.py:206
  503.0 3.5 gather.19
  506.5 6.6 %multiply_reduce_fusion = f32[128,2048]{1,0:T(8,128)} fusion(f32[128,2,2048]{2,1,0:T(2,128)} %gather.19, pred[128,2]{1,0:T(8,128)(4,1)S(1)} %copy.139, f32[128,2]{1,0:T(8,128)S(1)} %copy.142), kind=kLoop, calls=%fused_computation.42 | loop fusion | flops 1310720 | bytes 3147008 | tf_op jit(solution)/shard_map/reduce_sum | solution.py:207
  513.1 3.1 fusion.28
  (129 shorter events, 12.0 us)
Async XLA Ops:
  6.5 176.6 %copy-start = (bf16[4,128,2048]{2,1,0:T(8,128)(2,1)S(1)}, bf16[4,128,2048]{2,1,0:T(8,128)(2,1)}, u32[]{:S(2)}) copy-start(bf16[4,128,2048]{2,1,0:T(8,128)(2,1)} %param.22) | copy-start | bytes 6291460
  6.5 6.0 %copy-start.24 = (s32[32]{0:T(128)S(1)}, s32[32]{0:T(128)}, u32[]{:S(2)}) copy-start(s32[32]{0:T(128)} %param.24) | copy-start | bytes 388
  6.5 78.2 %all-gather.2.cloned.1.call-start = ((), (), s32[]{:S(2)}) async-start(), calls=%async_computation.5 | async-start | bytes 8912896 | tf_op jit(solution)/shard_map/all_gather | solution.py:118
  9.3 9.5 %copy-start.14 = (s32[2048,2]{0,1:T(2,128)S(1)}, s32[2048,2]{0,1:T(2,128)}, u32[]{:S(2)}) copy-start(s32[2048,2]{0,1:T(2,128)} %param.26) | copy-start | bytes 49156
  13.8 7.9 %copy-start.25 = (s32[1,4]{1,0:T(1,128)S(1)}, s32[1,4]{1,0:T(1,128)}, u32[]{:S(2)}) copy-start(s32[1,4]{1,0:T(1,128)} %param.25) | copy-start | bytes 52
  13.8 26.8 %all-to-all-start = ((bf16[8,128,1,256]{3,1,2,0:T(8,128)(2,1)}), bf16[8,128,1,256]{3,1,2,0:T(8,128)(2,1)}, u32[]{:S(2)}, u32[]{:S(2)}) async-start(bf16[8,128,1,256]{3,1,2,0:T(8,128)(2,1)} %copy.128), calls=%async_computation | async-start | bytes 1048576 | tf_op jit(solution)/shard_map/all_to_all | solution.py:105
  18.8 256.8 %reduce-scatter.2.cloned.1.call-start = ((), (), s32[]{:S(2)}) async-start(), calls=%async_computation.6 | async-start | bytes 8912896 | tf_op jit(solution)/shard_map/reduce_scatter | solution.py:170
  22.0 14.4 %copy-start.11 = (s32[2048]{0:T(1024)}, s32[2048]{0:T(1024)S(1)}, u32[]{:S(2)}) copy-start(s32[2048]{0:T(1024)S(1)} %convert_reduce_fusion.1) | copy-start | bytes 24580
  31.4 2.8 copy-start.16
  34.2 50.5 %copy-start.8 = (bf16[256,2048]{1,0:T(8,128)(2,1)S(1)}, bf16[256,2048]{1,0:T(8,128)(2,1)}, u32[]{:S(2)}) copy-start(bf16[256,2048]{1,0:T(8,128)(2,1)} %copy.130) | copy-start | bytes 3145732
  35.6 6.7 %copy-start.20 = (f32[64]{0:T(128)}, f32[64]{0:T(128)S(1)}, u32[]{:S(2)}) copy-start(f32[64]{0:T(128)S(1)} %multiply_power_fusion) | copy-start | bytes 772
  36.5 5.8 %copy-start.12 = (f32[2048]{0:T(1024)}, f32[2048]{0:T(1024)S(1)}, u32[]{:S(2)}) copy-start(f32[2048]{0:T(1024)S(1)} %subtract_convert_fusion.1) | copy-start | bytes 24580
  84.8 7.8 %copy-start.23 = (bf16[2048,2048]{1,0:T(8,128)(2,1)S(1)}, bf16[2048,2048]{1,0:T(8,128)(2,1)}, u32[]{:S(2)}) copy-start(bf16[2048,2048]{1,0:T(8,128)(2,1)} %all-gather.2.cloned.1.call-done) | copy-start | bytes 25165828
  90.7 2.0 copy-start.5
  92.6 4.5 copy-start.3
  92.6 4.5 copy-start.4
  105.4 5.5 %copy-start.6 = (bf16[2048,1,128]{0,2,1:T(8,128)(2,1)S(1)}, bf16[2048,1,128]{0,2,1:T(8,128)(2,1)}, u32[]{:S(2)}) copy-start(bf16[2048,1,128]{0,2,1:T(8,128)(2,1)} %fusion.52) | copy-start | bytes 1572868
  112.1 4.7 copy-start.15
  116.8 13.0 %copy-start.17 = (pred[4,1024]{1,0:T(4,128)(4,1)S(1)}, pred[4,1024]{1,0:T(4,128)(4,1)}, u32[]{:S(2)}) copy-start(pred[4,1024]{1,0:T(4,128)(4,1)} %compare_and_fusion) | copy-start | bytes 12292
  116.8 15.1 %copy-start.18 = (s32[2560]{0:T(1024)S(1)}, s32[2560]{0:T(1024)}, u32[]{:S(2)}) copy-start(s32[2560]{0:T(1024)} %pad_add_fusion) | copy-start | bytes 30724
  116.8 15.1 %copy-start.26 = (s32[2560]{0:T(1024)S(1)}, s32[2560]{0:T(1024)}, u32[]{:S(2)}) copy-start(s32[2560]{0:T(1024)} %constant.115.clone.1) | copy-start | bytes 30724
  131.9 37.0 %copy-start.7 = (s32[2048,2]{1,0:T(8,128)S(1)}, s32[2048,2]{1,0:T(8,128)}, u32[]{:S(2)}) copy-start(s32[2048,2]{1,0:T(8,128)} %copy.119) | copy-start | bytes 49156
  136.7 1.6 copy-start.9
  145.9 1.6 copy-start.9
  155.1 1.6 copy-start.9
  164.4 1.6 copy-start.9
  189.7 0.7 copy-start.19
  189.7 85.8 %copy-start.1 = (bf16[128,2048]{1,0:T(8,128)(2,1)S(1)}, bf16[128,2048]{1,0:T(8,128)(2,1)}, u32[]{:S(2)}) copy-start(bf16[128,2048]{1,0:T(8,128)(2,1)} %param.18) | copy-start | bytes 1572868
  189.7 87.1 %copy-start.13 = (f32[1,2048]{1,0:T(1,128)S(1)}, f32[1,2048]{1,0:T(1,128)}, u32[]{:S(2)}) copy-start(f32[1,2048]{1,0:T(1,128)} %get-tuple-element.158) | copy-start | bytes 24580
  278.8 37.4 %copy-start.10 = (bf16[4,2,16,2048]{3,2,1,0:T(8,128)(2,1)S(1)}, bf16[4,2,16,2048]{3,2,1,0:T(8,128)(2,1)}, u32[]{:S(2)}) copy-start(bf16[4,2,16,2048]{3,2,1,0:T(8,128)(2,1)} %param.32) | copy-start | bytes 1572868
  320.5 132.1 %all-to-all-start.3 = ((bf16[16,4,2,16,2048]{4,3,2,1,0:T(8,128)(2,1)}), bf16[16,4,2,16,2048]{4,3,2,1,0:T(8,128)(2,1)}, u32[]{:S(2)}, u32[]{:S(2)}) async-start(bf16[16,4,2,16,2048]{4,3,2,1,0:T(8,128)(2,1)} %stack.2), calls=%async_computation.4 | async-start | bytes 16777216 | tf_op jit(solution)/shard_map/all_to_all | solution.py:83
  347.3 115.3 %copy-start.21 = (f32[128,2]{0,1:T(2,128)S(1)}, f32[128,2]{0,1:T(2,128)}, u32[]{:S(2)}) copy-start(f32[128,2]{0,1:T(2,128)} %param.31) | copy-start | bytes 3076
  347.3 116.2 %copy-start.22 = (s32[32]{0:T(128)S(1)}, s32[32]{0:T(128)}, u32[]{:S(2)}) copy-start(s32[32]{0:T(128)} %param.33) | copy-start | bytes 388
  452.7 40.9 %all-to-all-start.2 = ((bf16[16,40,2048]{2,1,0:T(8,128)(2,1)}), bf16[16,40,2048]{2,1,0:T(8,128)(2,1)}, u32[]{:S(2)}, u32[]{:S(2)}) async-start(bf16[16,40,2048]{2,1,0:T(8,128)(2,1)} %fusion.21), calls=%async_computation.3 | async-start | bytes 5242880 | tf_op jit(solution)/shard_map/all_to_all | solution.py:200
  506.5 6.6 %copy-start.2 = (bf16[128,2048]{1,0:T(8,128)(2,1)S(1)}, bf16[128,2048]{1,0:T(8,128)(2,1)}, u32[]{:S(2)}) copy-start(bf16[128,2048]{1,0:T(8,128)(2,1)} %reduce-scatter.2.cloned.1.call-done) | copy-start | bytes 1572868
Sparse Core Ops, SparseCore 0:
  11.5 73.2 all-gather.1
  189.9 85.6 reduce-scatter.1
